TPU v7x, 32 devices: a whole 2x2x4 slice. The times are simulated.
32 devices in a mesh: rec: 4 (over y, x), win: 8 (over z, core).
Axes of the slice: x: 2, y: 2, z: 4, core: 2. Of those that a mesh axis runs over, the one named last changes fastest.
Arguments:
- strain: bfloat16 [1024, 32, 2176], P('rec', 'win'), may hold values from -90 to 90
- sources: int32 [256], replicated, may hold values from 0 to 1023, as said below
- offsets: int32 [32], P('win'), may hold values from 0 to 128
Outputs:
- cross: bfloat16 [2, 256, 512, 1024], P(None, None, 'win', 'rec')
Inputs may be any that keep to these rules, and one draw needn't show every extreme that they name: sources are distinct; among the channels i * 256 to (i + 1) * 256 - 1 of any i there are at most 128 of them, and exactly 128 for some i.
All inputs are finite; a program needn't handle non-finite values.
Results may differ from a plain program's by a relative error of at most 0.0057.
Values may be sent and summed in bfloat16 or wider, within the bound.
No kernel may reach another device: no remote copies, remote signals or barrier semaphores. Data moves between devices by JAX's collectives and lax.ppermute only.
A program may use at most 128 MiB of HBM per device.

v0:
```python
import math

import jax
import jax.numpy as jnp
from jax import lax
from jax.sharding import PartitionSpec as P

NT = 2048
NF = 512
F_LO = 10
SUB = 64


EPSILON = 1e-06


def cut_records(strain, offsets, length):

    def one_record(trace_rows, begin_at):
        return lax.dynamic_slice_in_dim(trace_rows, begin_at, length, 1)

    return jax.vmap(one_record, in_axes=(1, 0))(strain, offsets)


def taper_window(length):
    edge = length // 16
    sample = jnp.arange(length, dtype=jnp.float32)
    rising = 0.5 * (1.0 - jnp.cos(math.pi * (sample + 0.5) / edge))
    falling = 0.5 * (1.0 - jnp.cos(math.pi * (length - sample - 0.5) / edge))
    return jnp.where(sample < edge, rising, jnp.where(sample >= length - edge, falling, 1.0))


def dft_table(length, first_bin, count):
    freq = first_bin + jnp.arange(count, dtype=jnp.int32)
    sample = jnp.arange(length, dtype=jnp.int32)
    phase = (freq[:, None] * sample[None, :] % length).astype(jnp.float32) * (
        2.0 * math.pi / length
    )
    return jnp.stack((jnp.cos(phase), -jnp.sin(phase)))


def whiten(spectra):
    dims = spectra.shape
    blocks = spectra.reshape(dims[0], dims[1] // SUB, SUB, dims[2], dims[3])
    power = jnp.mean(blocks[0] * blocks[0] + blocks[1] * blocks[1], axis=1, keepdims=True)
    return (blocks * lax.rsqrt(power + EPSILON)).reshape(dims).astype(jnp.bfloat16)


def body(strain, sources, offsets):
    records = cut_records(strain, offsets, NT).astype(jnp.float32)
    centred = records - jnp.mean(records, axis=-1, keepdims=True)
    tapered = centred * taper_window(NT)
    table = dft_table(NT, F_LO, NF)
    spectra = jnp.einsum(
        "qjt,rct->qjrc",
        table,
        tapered,
        precision=lax.Precision.HIGH,
        preferred_element_type=jnp.float32,
    )
    white = whiten(spectra)
    chan_dev = strain.shape[0]
    local = sources - lax.axis_index("rec") * chan_dev
    owned = (local >= 0) & (local < chan_dev)
    column = jnp.clip(local, 0, chan_dev - 1)
    keeper = owned.astype(jnp.bfloat16)
    banded = lax.all_to_all(white, "win", split_axis=1, concat_axis=2, tiled=True)
    picked = jnp.take(banded, column, axis=3) * keeper
    source_spec = lax.psum(picked.astype(jnp.float32).astype(jnp.bfloat16), "rec")
    record_total = banded.shape[2]
    turned = jnp.stack((source_spec[1], -source_spec[0]))
    real_part = jnp.einsum(
        "qfrs,qfrc->sfc", source_spec, banded, preferred_element_type=jnp.float32
    )
    imag_part = jnp.einsum("qfrs,qfrc->sfc", turned, banded, preferred_element_type=jnp.float32)
    return (jnp.stack((real_part, imag_part)) / record_total).astype(jnp.bfloat16)


def solution(mesh):
    placed = (P("rec", "win", None), P(), P("win"))
    return jax.shard_map(
        body, mesh=mesh, in_specs=placed, out_specs=P(None, None, "win", "rec"), check_vma=False
    )
```

profile of v0, /device:TPU:0, one launch (start us, length us, event | category | flops | bytes accessed | tf_op | source)
XLA Modules:
  0.0 291.9 jit_solution(16698834517380342040)
XLA Ops:
  6.6 0.7 fusion.30
  7.4 4.9 %copy.26 = bf16[256,4,2176]{2,0,1:T(8,128)(2,1)} copy(bf16[256,4,2176]{2,1,0:T(4,128)(2,1)} %param.3) | data formatting | bytes 8912896 | tf_op args[0]
  12.3 18.0 %while.1 = (s32[]{:T(128)}, bf16[4,256,2176]{2,1,0:T(8,128)(2,1)}, s32[4,3]{1,0:T(4,128)S(1)}, bf16[4,256,2048]{2,1,0:T(8,128)(2,1)}, s32[]{:T(128)}) while((s32[]{:T(128)}, bf16[4,256,2176]{2,1,0:T(8,128)(2,1)}, s32[4,3]{1,0:T(4,128)S(1)}, bf16[4,256,2048]{2,1,0:T(8,128)(2,1)}, s32[]{:T(128)}) %tuple.31), condition=%wide.while_cond, body=%wide.while_body.sunk | while | flops 2 | bytes 2098293 | solution.py:20
  12.3 0.6 fusion.39
  12.9 3.9 %dynamic-slice_dynamic-update-slice_fusion.2 = bf16[4,256,2048]{2,1,0:T(8,128)(2,1)} fusion(bf16[4,256,2048]{2,1,0:T(8,128)(2,1)} %get-tuple-element.79, s32[]{:T(128)S(6)} %copy.31, bf16[4,256,2176]{2,1,0:T(8,128)(2,1)} %get-tuple-element.82, s32[]{:T(128)} %bitcast.44, s32[]{:T(128)} %bitcast.45), kind=kLoop, calls=%fused_computation.1.clone.1 | loop fusion | bytes 2098180 | tf_op jit(solution)/shard_map/vmap()/gather
  16.8 0.6 fusion.39
  17.4 3.9 %dynamic-slice_dynamic-update-slice_fusion.2 = bf16[4,256,2048]{2,1,0:T(8,128)(2,1)} fusion(bf16[4,256,2048]{2,1,0:T(8,128)(2,1)} %get-tuple-element.79, s32[]{:T(128)S(6)} %copy.31, bf16[4,256,2176]{2,1,0:T(8,128)(2,1)} %get-tuple-element.82, s32[]{:T(128)} %bitcast.44, s32[]{:T(128)} %bitcast.45), kind=kLoop, calls=%fused_computation.1.clone.1 | loop fusion | bytes 2098180 | tf_op jit(solution)/shard_map/vmap()/gather
  21.3 0.6 fusion.39
  21.9 3.9 %dynamic-slice_dynamic-update-slice_fusion.2 = bf16[4,256,2048]{2,1,0:T(8,128)(2,1)} fusion(bf16[4,256,2048]{2,1,0:T(8,128)(2,1)} %get-tuple-element.79, s32[]{:T(128)S(6)} %copy.31, bf16[4,256,2176]{2,1,0:T(8,128)(2,1)} %get-tuple-element.82, s32[]{:T(128)} %bitcast.44, s32[]{:T(128)} %bitcast.45), kind=kLoop, calls=%fused_computation.1.clone.1 | loop fusion | bytes 2098180 | tf_op jit(solution)/shard_map/vmap()/gather
  25.8 0.6 fusion.39
  26.4 3.9 %dynamic-slice_dynamic-update-slice_fusion.2 = bf16[4,256,2048]{2,1,0:T(8,128)(2,1)} fusion(bf16[4,256,2048]{2,1,0:T(8,128)(2,1)} %get-tuple-element.79, s32[]{:T(128)S(6)} %copy.31, bf16[4,256,2176]{2,1,0:T(8,128)(2,1)} %get-tuple-element.82, s32[]{:T(128)} %bitcast.44, s32[]{:T(128)} %bitcast.45), kind=kLoop, calls=%fused_computation.1.clone.1 | loop fusion | bytes 2098180 | tf_op jit(solution)/shard_map/vmap()/gather
  30.3 2.8 convert_reduce_fusion
  33.1 17.0 %fusion.19 = (f32[1,512,2048]{2,1,0:T(8,128)S(1)}, f32[1,512,2048]{2,1,0:T(8,128)S(1)}) fusion(s32[512]{0:T(512)S(1)} %iota_add_fusion.1), kind=kLoop, calls=%fused_computation.37 | loop fusion | flops 15728640 | bytes 8390656 | tf_op jit(solution)/shard_map/cos | solution.py:39
  50.1 13.4 %fusion.3 = f32[2,512,4,256]{3,1,2,0:T(8,128)S(1)} fusion(bf16[4,256,2048]{2,1,0:T(8,128)(2,1)S(1)} %copy-done.2, f32[1,512,2048]{2,1,0:T(8,128)S(1)} %get-tuple-element.40, f32[1,512,2048]{2,1,0:T(8,128)S(1)} %get-tuple-element.39, f32[2048]{0:T(1024)S(1)} %fusion.24, f32[4,256]{1,0:T(4,128)S(1)} %broadcast_multiply_fusion), kind=kOutput, calls=%fused_computation.11 | convolution fusion | flops 12893290496 | bytes 16789504 | tf_op jit(solution)/shard_map/qjt,rct->qjrc/dot_general | solution.py:54
  63.5 2.0 copy-done
  65.5 9.9 %fusion.15 = f32[1,512,4,256]{3,1,2,0:T(8,128)S(1)} fusion(f32[2,512,4,256]{3,1,2,0:T(8,128)S(1)} %fusion.3), kind=kLoop, calls=%fused_computation.30 | loop fusion | flops 1572864 | bytes 6291456 | tf_op jit(solution)/shard_map/add | solution.py:45
  75.8 2.8 multiply_convert_fusion
  78.6 2.9 %copy.16 = bf16[2,512,4,256]{3,2,0,1:T(4,128)(2,1)} copy(bf16[2,512,4,256]{3,1,2,0:T(8,128)(2,1)S(1)} %multiply_convert_fusion) | data formatting | bytes 4194304 | tf_op jit(solution)/shard_map/convert_element_type | solution.py:46
  81.5 6.4 %all-to-all-start = ((bf16[2,512,4,256]{3,2,0,1:T(4,128)(2,1)}), bf16[2,512,4,256]{3,2,0,1:T(4,128)(2,1)S(1)}, u32[]{:S(2)}, u32[]{:S(2)}) async-start(bf16[2,512,4,256]{3,2,0,1:T(4,128)(2,1)} %copy.16), calls=%async_computation | async-start | bytes 4194304 | tf_op jit(solution)/shard_map/all_to_all | solution.py:67
  88.0 48.9 %all-to-all-done = bf16[2,512,4,256]{3,2,0,1:T(4,128)(2,1)S(1)} async-done(((bf16[2,512,4,256]{3,2,0,1:T(4,128)(2,1)}), bf16[2,512,4,256]{3,2,0,1:T(4,128)(2,1)S(1)}, u32[]{:S(2)}, u32[]{:S(2)}) %all-to-all-start) | async-done | bytes 2097184 | tf_op jit(solution)/shard_map/all_to_all | solution.py:67
  136.9 2.5 copy.27
  139.4 2.5 all_to_all.16
  142.0 7.8 %copy.18 = bf16[2,64,32,256]{1,2,3,0:T(8,128)(2,1)} copy(bf16[2,64,32,256]{3,2,0,1:T(8,128)(2,1)S(1)} %all_to_all.16) | data formatting | bytes 4194304 | tf_op jit(solution)/shard_map/all_to_all | solution.py:67
  149.8 5.3 %gather_fusion = bf16[256,2,64,32]{2,3,1,0:T(8,128)(2,1)} fusion(bf16[2,64,32,256]{1,2,3,0:T(8,128)(2,1)} %copy.18, s32[1024]{0:T(1024)S(1)} %pad_clamp_fusion), kind=kCustom, calls=%fused_computation | custom fusion | bytes 4195328 | tf_op jit(solution)/shard_map/jit(_take)/gather | solution.py:68
  155.1 7.8 %copy.19 = bf16[256,2,64,32]{0,3,1,2:T(8,128)(2,1)} copy(bf16[256,2,64,32]{2,3,1,0:T(8,128)(2,1)} %gather_fusion) | data formatting | bytes 4194304 | tf_op jit(solution)/shard_map/jit(_take)/gather | solution.py:68
  162.8 3.1 %multiply_bitcast_fusion = bf16[2,64,32,256]{3,2,0,1:T(8,128)(2,1)} fusion(bf16[256,2,64,32]{0,3,1,2:T(8,128)(2,1)} %copy.19, pred[256]{0:T(512)(128)(4,1)S(1)} %get-tuple-element.33, bf16[256]{0:T(256)(128)(2,1)S(1)} %get-tuple-element.41), kind=kLoop, calls=%fused_computation.36 | loop fusion | flops 2097152 | bytes 4195072 | tf_op jit(solution)/shard_map/mul | solution.py:68
  165.9 68.6 %all-reduce.3.cloned.1.call-done = bf16[2,64,32,256]{3,2,0,1:T(8,128)(2,1)} async-done(((bf16[2,64,32,256]{3,2,0,1:T(8,128)(2,1)}), bf16[2,64,32,256]{3,2,0,1:T(8,128)(2,1)}) %all-reduce.3.cloned.1.call-update) | async-done | bytes 2097168 | tf_op jit(solution)/shard_map/psum | solution.py:69
  234.5 1.7 fusion.34
  236.2 2.4 convolution_bitcast_fusion
  238.6 8.5 %convolution_bitcast_fusion.1 = f32[1,256,64,256]{1,3,2,0:T(8,128)} fusion(bf16[2,64,32,256]{3,2,0,1:T(8,128)(2,1)S(1)} %all_to_all.16, bf16[2,64,32,256]{3,2,0,1:T(8,128)(2,1)S(1)} %copy-done.1), kind=kOutput, calls=%fused_computation.8 | convolution fusion | flops 536870912 | bytes 20971520 | tf_op jit(solution)/shard_map/qfrs,qfrc->sfc/dot_general | solution.py:72
  247.1 14.9 %fusion = bf16[2,256,64,256]{1,3,2,0:T(8,128)(2,1)} fusion(f32[1,256,64,256]{1,3,2,0:T(8,128)S(1)} %convolution_bitcast_fusion, f32[1,256,64,256]{1,3,2,0:T(8,128)} %convolution_bitcast_fusion.1), kind=kLoop, calls=%fused_computation.4 | loop fusion | flops 25165824 | bytes 50331648 | tf_op jit(solution)/shard_map/convert_element_type | solution.py:76
  262.0 22.8 %copy.20 = bf16[2,256,64,256]{3,2,1,0:T(8,128)(2,1)} copy(bf16[2,256,64,256]{1,3,2,0:T(8,128)(2,1)} %fusion) | data formatting | bytes 33554432 | tf_op jit(solution)/shard_map/convert_element_type | solution.py:76
  (25 shorter events, 0.7 us)
Async XLA Ops:
  33.1 17.0 %copy-start.2 = (bf16[4,256,2048]{2,1,0:T(8,128)(2,1)S(1)}, bf16[4,256,2048]{2,1,0:T(8,128)(2,1)}, u32[]{:S(2)}) copy-start(bf16[4,256,2048]{2,1,0:T(8,128)(2,1)} %get-tuple-element.12) | copy-start | bytes 12582916
  63.5 2.0 copy-start
  78.6 9.4 %copy-start.3 = (s32[256]{0:T(256)S(1)}, s32[256]{0:T(256)}, u32[]{:S(2)}) copy-start(s32[256]{0:T(256)} %param.4) | copy-start | bytes 3076
  81.5 55.4 %all-to-all-start = ((bf16[2,512,4,256]{3,2,0,1:T(4,128)(2,1)}), bf16[2,512,4,256]{3,2,0,1:T(4,128)(2,1)S(1)}, u32[]{:S(2)}, u32[]{:S(2)}) async-start(bf16[2,512,4,256]{3,2,0,1:T(4,128)(2,1)} %copy.16), calls=%async_computation | async-start | bytes 4194304 | tf_op jit(solution)/shard_map/all_to_all | solution.py:67
  87.9 146.6 %all-reduce.3.cloned.1.call-start = ((), (), s32[]{:S(2)}) async-start(), calls=%async_computation.1 | async-start | bytes 4194304 | tf_op jit(solution)/shard_map/psum | solution.py:69
  236.2 2.4 copy-start.1
Sparse Core Ops, SparseCore 0:
  166.1 68.3 all-reduce.2
where the time goes:
time: 296 us; the launch traced here: 292 us
  waiting for transfers between devices  118 us (40%)
  local copies, waits for them, and re-layouts  76.8 us (26%)
  other arithmetic  53.1 us (18%)
  matrix products  24.3 us (8%)
  between operations  13.8 us (5%)
  starting transfers between devices  6.41 us (2%)
    psum x1, waiting for transfers between devices, body(): lax.psum(picked.astype(jnp.float32).astype(jnp.bfloat16), 'rec')  68.6 us
    all_to_all x1, waiting for transfers between devices, body(): lax.all_to_all(white, 'win', split_axis=1, concat_axis=2, tiled=True)  48.9 us
    convert_element_type x1, local copies, waits for them, and re-layouts, body(): (jnp.stack((real_part, imag_part)) / record_total).astype(jnp.bfloat16)  22.8 us
    gather x12, local copies, waits for them, and re-layouts  18 us
    cos x1, other arithmetic, dft_table(): return jnp.stack((jnp.cos(phase), -jnp.sin(phase)))  17 us
    convert_element_type x1, other arithmetic, body(): (jnp.stack((real_part, imag_part)) / record_total).astype(jnp.bfloat16)  14.9 us
    dot_general x1, matrix products, body(): jnp.einsum('qjt,rct->qjrc', table, tapered, precision=lax.Precision.HIGH,...  13.4 us
    gather x2, local copies, waits for them, and re-layouts, body(): picked = jnp.take(banded, column, axis=3) * keeper  13 us
  transfers between devices with their start and end apart: 2, of which 2 were waited for; matrix products, arithmetic and copies ran while one was open for 0% of the time, Pallas kernels for 0%

commit v1 on v0

v1 whole, which is shorter than its diff:
```python
import functools
import math

import jax
import jax.numpy as jnp
import numpy as np
from jax import lax
from jax.experimental import pallas as pl
from jax.experimental.pallas import tpu as pltpu
from jax.sharding import PartitionSpec as P

NT = 2048
NF = 512
F_LO = 10
SUB = 64
HALF = NT // 2
LANES = 128
NBAND = NF // SUB
PAIRS = SUB // 2
CHUNKS = 2
JBLOCK = 16

EPSILON = 1e-06

NT_DIMS = (((1,), (1,)), ((), ()))


def table_parts():
    pair = np.arange(PAIRS)
    band = np.arange(NBAND)
    beta_sample = np.arange(LANES)
    fine = np.zeros((2, 2, NBAND, PAIRS, LANES), np.float64)
    coarse = np.zeros((2, 2, 2, 8, HALF), np.float64)
    row = np.arange(8)
    step = np.arange(HALF) // LANES
    for parity in range(2):
        bins = F_LO + band[:, None] * SUB + 2 * pair[None, :] + parity
        beta = 2.0 * np.pi * (bins[..., None] * beta_sample % NT) / NT
        fine[0, parity], fine[1, parity] = np.cos(beta), np.sin(beta)
        turns = (F_LO + 2 * row + parity)[:, None] * step[None, :] % 16
        for part in range(2):
            alpha = 2.0 * np.pi * turns / 16.0 + part * np.pi / 2.0
            coarse[0, parity, part], coarse[1, parity, part] = np.cos(alpha), np.sin(alpha)
    return fine.astype(np.float32), coarse.astype(np.float32)


def front_kernel(rows_dev, wins, offs, strain, perm, fine, coarse, *rest):
    outs = rest[: 2 * CHUNKS]
    high, low, table_high, table_low, spec, laid = rest[2 * CHUNKS :]
    chan, _, seg = strain.shape
    bins_dev = NF // wins

    for parity in range(2):
        for part in range(2):
            for step in range(HALF // LANES):
                at = pl.ds(step * LANES, LANES)
                cos_a = coarse[0, parity, part, :, at]
                sin_a = coarse[1, parity, part, :, at]
                cos_b = fine[0, parity].reshape(NBAND * PAIRS // 8, 8, LANES)
                sin_b = fine[1, parity].reshape(NBAND * PAIRS // 8, 8, LANES)
                value = (cos_a[None] * cos_b - sin_a[None] * sin_b).reshape(NBAND, PAIRS, LANES)
                top = value.astype(jnp.bfloat16)
                table_high[parity, :, pl.ds(part * PAIRS, PAIRS), at] = top
                table_low[parity, :, pl.ds(part * PAIRS, PAIRS), at] = (
                    value - top.astype(jnp.float32)
                ).astype(jnp.bfloat16)

    edge = NT // 16
    place = lax.broadcasted_iota(jnp.int32, (8, seg), 1)
    number = lax.broadcasted_iota(jnp.int32, (8, seg), 0)
    begin = jnp.zeros((8, seg), jnp.int32)
    for r in range(rows_dev):
        begin = jnp.where(number == r, offs[r], begin)
    sample = place - begin
    inside = (sample >= 0) & (sample < NT)
    near = jnp.minimum(sample, NT - 1 - sample).astype(jnp.float32) + 0.5
    slope = 0.5 * (1.0 - jnp.cos(near * (math.pi / edge)))
    taper = jnp.where(inside, jnp.where(near < edge, slope, 1.0), 0.0)
    window = jnp.where(inside, 1.0, 0.0)

    step_rows = 16

    def prepare(i, carry):
        at = pl.ds(pl.multiple_of(i * step_rows, step_rows), step_rows)
        for r in range(rows_dev):
            x = strain[at, r, :].astype(jnp.float32)
            mean = jnp.sum(x * window[r : r + 1], axis=1, keepdims=True) * (1.0 / NT)
            z = (x - mean) * taper[r : r + 1]
            first = jnp.concatenate((z[:, : seg - NT] + z[:, NT:], z[:, seg - NT : HALF]), axis=1)
            second = z[:, HALF:NT]
            for parity, folded in enumerate((first + second, first - second)):
                top = folded.astype(jnp.bfloat16)
                high[r, parity, at, :] = top
                low[r, parity, at, :] = (folded - top.astype(jnp.float32)).astype(jnp.bfloat16)
        return carry

    lax.fori_loop(0, chan // step_rows, prepare, 0)

    rows = NBAND * SUB
    for r in range(rows_dev):
        for parity in range(2):
            t_high = table_high[parity].reshape(rows, HALF)
            t_low = table_low[parity].reshape(rows, HALF)
            x_high, x_low = high[r, parity], low[r, parity]
            dot = functools.partial(
                lax.dot_general, dimension_numbers=NT_DIMS, preferred_element_type=jnp.float32
            )
            spec[parity] = dot(t_high, x_high) + dot(t_high, x_low) + dot(t_low, x_high)

        off = offs[r]
        pair = lax.broadcasted_iota(jnp.int32, (PAIRS, LANES), 0)
        turn = 2.0 * math.pi / NT
        inner = []
        for parity in range(2):
            angle = (((F_LO + 2 * pair + parity) * off) & (NT - 1)).astype(jnp.float32) * turn
            inner.append((jnp.cos(angle), jnp.sin(angle)))
        band_no = lax.broadcasted_iota(jnp.int32, (NBAND, LANES), 0)
        angle = ((SUB * band_no * off) & (NT - 1)).astype(jnp.float32) * turn
        band_cos, band_sin = jnp.cos(angle), jnp.sin(angle)

        for band in range(NBAND):
            total = None
            for parity in range(2):
                block = spec[parity, pl.ds(band * SUB, SUB), :]
                energy = jnp.sum(block * block, axis=0, keepdims=True)
                total = energy if total is None else total + energy
            scale = lax.rsqrt(total * (1.0 / SUB) + EPSILON)
            bc, bs = band_cos[band : band + 1], band_sin[band : band + 1]
            for parity in range(2):
                ic, is_ = inner[parity]
                cos = ic * bc - is_ * bs
                sin = ic * bs + is_ * bc
                for lane in range(chan // LANES):
                    lanes = pl.ds(lane * LANES, LANES)
                    scale_l = scale[:, lane * LANES : (lane + 1) * LANES]
                    real = spec[parity, pl.ds(band * SUB, PAIRS), lanes] * scale_l
                    imag = spec[parity, pl.ds(band * SUB + PAIRS, PAIRS), lanes] * scale_l
                    for part, value in enumerate((real * cos - imag * sin, real * sin + imag * cos)):
                        start = band * SUB * 2 * rows_dev + parity * 2 * rows_dev + part * rows_dev + r
                        laid[lane, pl.ds(start, PAIRS, stride=4 * rows_dev), :] = value

    per_win = bins_dev * 2 * rows_dev
    per_chunk = per_win // CHUNKS

    def emit(w, carry):
        at = pl.ds(pl.multiple_of(w * per_win, per_win), per_win)
        white = jnp.concatenate(
            [laid[lane, at, :].astype(jnp.bfloat16) for lane in range(chan // LANES)], axis=1
        )
        placed = jnp.dot(white, perm[...], preferred_element_type=jnp.float32).astype(jnp.bfloat16)
        for k in range(CHUNKS):
            piece = placed[k * per_chunk : (k + 1) * per_chunk]
            for half in range(2):
                outs[2 * k + half][w] = piece[:, half * LANES : (half + 1) * LANES]
        return carry

    lax.fori_loop(0, wins, emit, 0)


def front(strain, offsets, perm, wins):
    chan, rows_dev, seg = strain.shape
    rows = NF // wins * 2 * rows_dev // CHUNKS
    fine, coarse = table_parts()
    vmem = pl.BlockSpec(memory_space=pltpu.VMEM)
    return pl.pallas_call(
        functools.partial(front_kernel, rows_dev, wins),
        out_shape=[jax.ShapeDtypeStruct((wins, rows, LANES), jnp.bfloat16)] * (2 * CHUNKS),
        in_specs=[pl.BlockSpec(memory_space=pltpu.SMEM)] + [vmem] * 4,
        out_specs=[vmem] * (2 * CHUNKS),
        scratch_shapes=[
            pltpu.VMEM((rows_dev, 2, chan, HALF), jnp.bfloat16),
            pltpu.VMEM((rows_dev, 2, chan, HALF), jnp.bfloat16),
            pltpu.VMEM((2, NBAND, SUB, HALF), jnp.bfloat16),
            pltpu.VMEM((2, NBAND, SUB, HALF), jnp.bfloat16),
            pltpu.VMEM((2, NBAND * SUB, chan), jnp.float32),
            pltpu.VMEM((chan // LANES, NF * 2 * rows_dev, LANES), jnp.float32),
        ],
        compiler_params=pltpu.CompilerParams(vmem_limit_bytes=56 * 2**20),
        name="front",
    )(offsets, strain, perm, jnp.asarray(fine), jnp.asarray(coarse))


def cross_kernel(rows_dev, wins, records, *refs):
    owners_refs, (other, perm, select), out, laid = refs[:-5], refs[-5:-2], refs[-2], refs[-1]
    mine = owners_refs[0]
    columns = select.shape[1] // LANES
    owners_refs = owners_refs[-columns:]
    depth = 2 * rows_dev * wins
    group = 256 // depth
    near = 2 * rows_dev * group
    width = wins * near
    sources = select.shape[0]
    scale = 1.0 / records

    lane = lax.broadcasted_iota(jnp.int32, (1, width), 1)
    row_no = lax.broadcasted_iota(jnp.int32, (width, width), 0)
    col_no = lax.broadcasted_iota(jnp.int32, (width, width), 1)
    first = (col_no // rows_dev) % 2 == 0
    turn = jnp.where(
        first & (row_no == col_no + rows_dev),
        1.0,
        jnp.where(jnp.logical_not(first) & (row_no == col_no - rows_dev), -1.0, 0.0),
    ).astype(jnp.bfloat16)
    keep = [((lane // (2 * rows_dev)) % group == b).astype(jnp.bfloat16) for b in range(group)]

    for g in range(JBLOCK // group):
        at = pl.ds(g * near, near)

        def rows_of(ref):
            return ref[:, at, :].reshape(width, LANES)

        slots = jnp.concatenate((rows_of(mine), rows_of(other)), axis=1)
        receivers = lax.dot_general(
            slots, perm[...], NT_DIMS, preferred_element_type=jnp.float32
        ).astype(jnp.bfloat16)
        held = jnp.concatenate([rows_of(ref) for ref in owners_refs], axis=1)
        picked = lax.dot_general(
            select[...], held, NT_DIMS, preferred_element_type=jnp.float32
        ).astype(jnp.bfloat16)
        turned = jnp.dot(picked, turn, preferred_element_type=jnp.float32).astype(jnp.bfloat16)
        for b in range(group):
            both = jnp.concatenate((picked * keep[b], turned * keep[b]), axis=0)
            product = jnp.dot(both, receivers, preferred_element_type=jnp.float32)
            for part in range(2):
                for half in range(product.shape[1] // LANES):
                    laid[part, half, pl.ds(g * group + b, sources, stride=JBLOCK), :] = product[
                        part * sources : (part + 1) * sources, half * LANES : (half + 1) * LANES
                    ]

    few = 16

    def emit(i, carry):
        rows = pl.ds(pl.multiple_of(i * few * JBLOCK, few * JBLOCK), few * JBLOCK)
        at = pl.ds(pl.multiple_of(i * few, few), few)
        for part in range(2):
            for half in range(laid.shape[1]):
                value = (laid[part, half, rows, :] * scale).astype(jnp.bfloat16)
                out[part, at, :, half * LANES : (half + 1) * LANES] = value.reshape(few, JBLOCK, LANES)
        return carry

    lax.fori_loop(0, sources // few, emit, 0)


def cross(k, whole, owners, other, perm, select, shape, records, rows_dev):
    wins, rows, _ = other.shape
    sources, chan = shape[1], shape[3]
    per_block = JBLOCK * 2 * rows_dev
    steps = rows // per_block
    piece = pl.BlockSpec((wins, per_block, LANES), lambda g: (0, g, 0))
    fixed = lambda array: pl.BlockSpec(array.shape, lambda g: (0, 0))
    args = list(owners) + [other, perm, select]
    specs = [piece] * (len(owners) + 1) + [fixed(perm), fixed(select)]
    body = functools.partial(cross_kernel, rows_dev, wins, records)
    aliases = {}
    if whole is not None:
        inner, count = body, len(args)
        body = lambda *refs: inner(*refs[:count], *refs[count + 1 :])
        aliases = {count: 0}
        args.append(whole)
        specs.append(pl.BlockSpec(memory_space=pl.ANY))
    return pl.pallas_call(
        body,
        grid=(steps,),
        out_shape=jax.ShapeDtypeStruct(shape, jnp.bfloat16),
        in_specs=specs,
        out_specs=pl.BlockSpec((2, sources, JBLOCK, chan), lambda g: (0, 0, k * steps + g, 0)),
        scratch_shapes=[pltpu.VMEM((2, chan // LANES, sources * JBLOCK, LANES), jnp.float32)],
        input_output_aliases=aliases,
        compiler_params=pltpu.CompilerParams(vmem_limit_bytes=56 * 2**20),
        name=f"cross{k}",
    )(*args)


def body(recs, wins, strain, sources, offsets):
    chan, rows_dev, _ = strain.shape
    me = lax.axis_index("rec")
    channel = jnp.arange(chan, dtype=jnp.int32)
    local = sources - me * chan
    hit = jnp.any(local[None, :] == channel[:, None], axis=1).astype(jnp.int32)
    ahead = jnp.sum(jnp.where(channel[None, :] < channel[:, None], hit[None, :], 0), axis=1)
    slot = jnp.where(hit > 0, ahead, jnp.sum(hit) + channel - ahead)
    perm = (slot[:, None] == channel[None, :]).astype(jnp.bfloat16)
    owner = sources // chan
    rank = jnp.sum(
        (owner[None, :] == owner[:, None]) & (sources[None, :] < sources[:, None]), axis=1
    ).astype(jnp.int32)
    if recs == 4:
        order = me ^ jnp.arange(4, dtype=jnp.int32)
    else:
        order = jnp.arange(recs, dtype=jnp.int32)
    place = jnp.arange(LANES, dtype=jnp.int32)
    select = (
        (owner[:, None, None] == order[None, :, None]) & (rank[:, None, None] == place[None, None, :])
    ).astype(jnp.bfloat16).reshape(sources.shape[0], recs * LANES)

    pieces = front(strain, offsets, perm, wins)

    def swap(array, bit):
        return lax.ppermute(array, "rec", [(i, i ^ bit) for i in range(recs)])

    def spread(array):
        return lax.all_to_all(array, "win", split_axis=0, concat_axis=0, tiled=True)

    owners = []
    for k in range(CHUNKS):
        mine = spread(pieces[2 * k])
        if recs == 4:
            along_x, along_y = swap(mine, 1), swap(mine, 2)
            far = swap(along_x, 2) if k % 2 == 0 else swap(along_y, 1)
            owners.append((mine, along_x, along_y, far))
        else:
            gathered = lax.all_gather(mine, "rec", axis=0)
            owners.append((mine,) + tuple(gathered[i] for i in range(recs)))
    shape = (2, sources.shape[0], NF // wins, chan)
    whole = None
    for k in range(CHUNKS):
        other = spread(pieces[2 * k + 1])
        whole = cross(k, whole, owners[k], other, perm, select, shape, rows_dev * wins, rows_dev)
    return whole


def solution(mesh):
    recs, wins = mesh.shape["rec"], mesh.shape["win"]
    placed = (P("rec", "win", None), P(), P("win"))
    return jax.shard_map(
        functools.partial(body, recs, wins),
        mesh=mesh,
        in_specs=placed,
        out_specs=P(None, None, "win", "rec"),
        check_vma=False,
    )
```

time: 296 us -> 146 us (0.49); the launches traced: 292 us -> 145 us
  waiting for transfers between devices: 118 us -> 32.2 us
  local copies, waits for them, and re-layouts: 76.8 us -> 2.53 us
  Pallas kernels: 0 us -> 51.3 us
  other arithmetic: 53.1 us -> 4.49 us
  blocking collectives: 0 us -> 40.4 us
  matrix products: 24.3 us -> 0 us
  between operations: 13.8 us -> 0.12 us
  starting transfers between devices: 6.41 us -> 14.4 us
    psum x1 -> x0, waiting for transfers between devices: 68.6 us -> none  [body(): lax.psum(picked.astype(jnp.float32).astype(jnp.bfloat16), 'rec')]
    pallas_call x0 -> x3, Pallas kernels: none -> 51.3 us  [the longest x2 27.6 us: cross(): pl.pallas_call(body, grid=(steps,), out_shape=jax.ShapeDtypeStruct(shape,...]
    all_to_all x0 -> x2, blocking collectives: none -> 40.4 us  [spread(): return lax.all_to_all(array, 'win', split_axis=0, concat_axis=0, tiled=True)]
    all_to_all x1 -> x2, waiting for transfers between devices: 48.9 us -> 12.2 us  [spread(): return lax.all_to_all(array, 'win', split_axis=0, concat_axis=0, tiled=True)]
    gather x14 -> x0, local copies, waits for them, and re-layouts: 31 us -> none
    convert_element_type x2 -> x0, local copies, waits for them, and re-layouts: 25.8 us -> none  [the longest x1 22.8 us: body(): (jnp.stack((real_part, imag_part)) / record_total).astype(jnp.bfloat16)]
    dot_general x3 -> x0, matrix products: 24.3 us -> none  [the longest x1 13.4 us: body(): jnp.einsum('qjt,rct->qjrc', table, tapered, precision=lax.Precision.HIGH,...]
    ppermute x0 -> x6, waiting for transfers between devices: none -> 20 us  [swap(): return lax.ppermute(array, 'rec', [(i, i ^ bit) for i in range(recs)])]
  transfers between devices with their start and end apart: 2 -> 8, of which waited for: 2 -> 3; matrix products, arithmetic and copies ran while one was open for 0% -> 2% of each run, Pallas kernels for 0% -> 9%
where the time goes in v1:
time: 146 us; the launch traced here: 145 us
  Pallas kernels  51.3 us (35%)
  blocking collectives  40.4 us (28%)
  waiting for transfers between devices  32.2 us (22%)
  starting transfers between devices  14.4 us (10%)
  other arithmetic  4.49 us (3%)
  local copies, waits for them, and re-layouts  2.53 us (2%)
    all_to_all x2, blocking collectives, spread(): return lax.all_to_all(array, 'win', split_axis=0, concat_axis=0, tiled=True)  40.4 us
    pallas_call x2, Pallas kernels, cross(): pl.pallas_call(body, grid=(steps,), out_shape=jax.ShapeDtypeStruct(shape,...  27.6 us
    pallas_call x1, Pallas kernels, front(): pl.pallas_call(functools.partial(front_kernel, rows_dev, wins), out_shape...  23.7 us
    ppermute x6, waiting for transfers between devices, swap(): return lax.ppermute(array, 'rec', [(i, i ^ bit) for i in range(recs)])  20 us
    all_to_all x2, waiting for transfers between devices, spread(): return lax.all_to_all(array, 'win', split_axis=0, concat_axis=0, tiled=True)  12.2 us
    ppermute x6, starting transfers between devices, swap(): return lax.ppermute(array, 'rec', [(i, i ^ bit) for i in range(recs)])  7.2 us
    all_to_all x2, starting transfers between devices, spread(): return lax.all_to_all(array, 'win', split_axis=0, concat_axis=0, tiled=True)  7.16 us
  transfers between devices with their start and end apart: 8, of which 3 were waited for; matrix products, arithmetic and copies ran while one was open for 2% of the time, Pallas kernels for 9%

profile of v1, /device:TPU:0, one launch (start us, length us, event | category | flops | bytes accessed | tf_op | source)
XLA Modules:
  0.0 145.4 jit_solution(4838813326112690087)
XLA Ops:
  0.0 0.7 and_select_fusion
  0.7 0.1 fusion
  0.8 0.6 convert_reduce_fusion.1
  1.4 0.1 select_reduce_fusion
  1.6 0.7 compare_select_fusion
  2.2 0.8 fusion.1.perm.refs_5_
  3.0 23.7 %front.1 = (bf16[8,256,128]{2,1,0:T(8,128)(2,1)}, bf16[8,256,128]{2,1,0:T(8,128)(2,1)}, bf16[8,256,128]{2,1,0:T(8,128)(2,1)}, bf16[8,256,128]{2,1,0:T(8,128)(2,1)}) custom-call(s32[4]{0:T(128)} %offs.1, bf16[256,4,2176]{2,1,0:T(4,128)(2,1)} %strain.1, bf16[256,256]{1,0:T(8,128)(2,1)} %fusion.1.perm.refs_5_, f32[2,2,8,32,128]{4,3,2,1,0:T(8,128)} %constant.30.clone.fine, ...), custom_call_target="tpu_custom_call" | custom-call | tf_op jit(solution)/shard_map/front/pallas_call | solution.py:165
  26.7 21.7 %all_to_all.20.refs_0_ = bf16[8,256,128]{2,1,0:T(8,128)(2,1)S(1)} all-to-all(bf16[8,256,128]{2,1,0:T(8,128)(2,1)} %get-tuple-element.9), channel_id=1, replica_groups=mesh['rec'=4,'win'=8] {'win'}, dimensions={0} | all-to-all | bytes 1048576 | tf_op jit(solution)/shard_map/all_to_all | solution.py:302
  48.4 18.7 %all_to_all.21.refs_0_ = bf16[8,256,128]{2,1,0:T(8,128)(2,1)S(1)} all-to-all(bf16[8,256,128]{2,1,0:T(8,128)(2,1)} %get-tuple-element.11), channel_id=1, replica_groups=mesh['rec'=4,'win'=8] {'win'}, dimensions={0} | all-to-all | bytes 1048576 | tf_op jit(solution)/shard_map/all_to_all | solution.py:302
  67.1 3.5 %all-to-all-start.3 = ((bf16[8,256,128]{2,1,0:T(8,128)(2,1)}), bf16[8,256,128]{2,1,0:T(8,128)(2,1)S(1)}, u32[]{:S(2)}, u32[]{:S(2)}) async-start(bf16[8,256,128]{2,1,0:T(8,128)(2,1)} %get-tuple-element.12), calls=%async_computation.3 | async-start | bytes 1048576 | tf_op jit(solution)/shard_map/all_to_all | solution.py:302
  70.6 1.6 %collective-permute-start.3 = (bf16[8,256,128]{2,1,0:T(8,128)(2,1)S(1)}, bf16[8,256,128]{2,1,0:T(8,128)(2,1)}, u32[]{:S(2)}, u32[]{:S(2)}) collective-permute-start(bf16[8,256,128]{2,1,0:T(8,128)(2,1)S(1)} %all_to_all.21.refs_0_), channel_id=1, source_target_pairs={{0,8},{8,0},{16,24},{24,16},{1,9},{9,1},{17,25},{25,17},{2,10},{10... | collective-permute-start | bytes 1572872 | tf_op jit(solution)/shard_map/ppermute | solution.py:299
  72.2 1.5 %collective-permute-start.1 = (bf16[8,256,128]{2,1,0:T(8,128)(2,1)S(1)}, bf16[8,256,128]{2,1,0:T(8,128)(2,1)S(1)}, u32[]{:S(2)}, u32[]{:S(2)}) collective-permute-start(bf16[8,256,128]{2,1,0:T(8,128)(2,1)S(1)} %all_to_all.20.refs_0_), channel_id=1, source_target_pairs={{0,16},{8,24},{16,0},{24,8},{1,17},{9,25},{17,1},{25,9},{2,18},{10... | collective-permute-start | bytes 1572872 | tf_op jit(solution)/shard_map/ppermute | solution.py:299
  73.7 12.2 %all-to-all-done.3.refs_4_ = bf16[8,256,128]{2,1,0:T(8,128)(2,1)S(1)} async-done(((bf16[8,256,128]{2,1,0:T(8,128)(2,1)}), bf16[8,256,128]{2,1,0:T(8,128)(2,1)S(1)}, u32[]{:S(2)}, u32[]{:S(2)}) %all-to-all-start.3) | async-done | bytes 524320 | tf_op jit(solution)/shard_map/all_to_all | solution.py:302
  85.9 3.7 %all-to-all-start.1 = ((bf16[8,256,128]{2,1,0:T(8,128)(2,1)}), bf16[8,256,128]{2,1,0:T(8,128)(2,1)S(1)}, u32[]{:S(2)}, u32[]{:S(2)}) async-start(bf16[8,256,128]{2,1,0:T(8,128)(2,1)} %get-tuple-element.10), calls=%async_computation.1 | async-start | bytes 1048576 | tf_op jit(solution)/shard_map/all_to_all | solution.py:302
  89.5 1.0 convert_reduce_fusion
  90.5 0.1 iota_compare_fusion.3
  90.6 1.6 %collective-permute-start.4 = (bf16[8,256,128]{2,1,0:T(8,128)(2,1)S(1)}, bf16[8,256,128]{2,1,0:T(8,128)(2,1)S(1)}, u32[]{:S(2)}, u32[]{:S(2)}) collective-permute-start(bf16[8,256,128]{2,1,0:T(8,128)(2,1)S(1)} %all_to_all.21.refs_0_), channel_id=1, source_target_pairs={{0,16},{8,24},{16,0},{24,8},{1,17},{9,25},{17,1},{25,9},{2,18},{10... | collective-permute-start | bytes 1572872 | tf_op jit(solution)/shard_map/ppermute | solution.py:299
  92.2 1.5 %collective-permute-start = (bf16[8,256,128]{2,1,0:T(8,128)(2,1)S(1)}, bf16[8,256,128]{2,1,0:T(8,128)(2,1)S(1)}, u32[]{:S(2)}, u32[]{:S(2)}) collective-permute-start(bf16[8,256,128]{2,1,0:T(8,128)(2,1)S(1)} %all_to_all.20.refs_0_), channel_id=1, source_target_pairs={{0,8},{8,0},{16,24},{24,16},{1,9},{9,1},{17,25},{25,17},{2,10},{10... | collective-permute-start | bytes 1572872 | tf_op jit(solution)/shard_map/ppermute | solution.py:299
  93.7 0.0 collective-permute-done.3.refs_1_
  93.7 0.5 collective-permute-start.5
  94.2 0.0 collective-permute-done.1.refs_2_
  94.2 0.5 collective-permute-start.2
  94.8 0.1 broadcast_compare_fusion
  94.9 0.3 and_convert_fusion
  95.2 0.8 copy.9
  96.0 9.5 %collective-permute-done.4.refs_2_ = bf16[8,256,128]{2,1,0:T(8,128)(2,1)S(1)} collective-permute-done((bf16[8,256,128]{2,1,0:T(8,128)(2,1)S(1)}, bf16[8,256,128]{2,1,0:T(8,128)(2,1)S(1)}, u32[]{:S(2)}, u32[]{:S(2)}) %collective-permute-start.4) | collective-permute-done | bytes 524320 | tf_op jit(solution)/shard_map/ppermute | solution.py:299
  105.5 10.5 %collective-permute-done.5.refs_3_ = bf16[8,256,128]{2,1,0:T(8,128)(2,1)S(1)} collective-permute-done((bf16[8,256,128]{2,1,0:T(8,128)(2,1)}, bf16[8,256,128]{2,1,0:T(8,128)(2,1)S(1)}, u32[]{:S(2)}, u32[]{:S(2)}) %collective-permute-start.5) | collective-permute-done | bytes 524320 | tf_op jit(solution)/shard_map/ppermute | solution.py:299
  116.0 0.8 copy-done.7
  116.8 13.8 %cross0.1.refs_7_ = bf16[2,256,64,256]{3,2,1,0:T(8,128)(2,1)} custom-call(bf16[8,256,128]{2,1,0:T(8,128)(2,1)} %copy-done.2, bf16[8,256,128]{2,1,0:T(8,128)(2,1)} %collective-permute-done.3.refs_1_, bf16[8,256,128]{2,1,0:T(8,128)(2,1)} %copy-done.6, bf16[8,256,128]{2,1,0:T(8,128)(2,1)} %copy-done.7, bf16[8,256,128]{2,1,0:T(8,128)(2,1)} %copy-done.3, ...), custom_call_target="tpu_custom_call" | custom-call | tf_op jit(solution)/shard_map/cross0/pallas_call | solution.py:261
  130.6 0.8 copy-done.1
  131.4 0.2 copy-done.5
  131.6 13.8 %cross1.1 = bf16[2,256,64,256]{3,2,1,0:T(8,128)(2,1)} custom-call(bf16[8,256,128]{2,1,0:T(8,128)(2,1)} %copy-done, bf16[8,256,128]{2,1,0:T(8,128)(2,1)} %copy-done.5, bf16[8,256,128]{2,1,0:T(8,128)(2,1)} %copy-done.4, bf16[8,256,128]{2,1,0:T(8,128)(2,1)} %collective-permute-done.2.refs_3_, ...), custom_call_target="tpu_custom_call", output_to_operand_aliasing={{}: (7, {})} | custom-call | tf_op jit(solution)/shard_map/cross1/pallas_call | solution.py:261
  (18 shorter events, 0.0 us)
Async XLA Ops:
  48.4 82.2 %copy-start = (bf16[8,256,128]{2,1,0:T(8,128)(2,1)}, bf16[8,256,128]{2,1,0:T(8,128)(2,1)S(1)}, u32[]{:S(2)}) copy-start(bf16[8,256,128]{2,1,0:T(8,128)(2,1)S(1)} %all_to_all.20.refs_0_) | copy-start | bytes 1572868
  67.1 48.9 %copy-start.2 = (bf16[8,256,128]{2,1,0:T(8,128)(2,1)}, bf16[8,256,128]{2,1,0:T(8,128)(2,1)S(1)}, u32[]{:S(2)}) copy-start(bf16[8,256,128]{2,1,0:T(8,128)(2,1)S(1)} %all_to_all.21.refs_0_) | copy-start | bytes 1572868
  67.1 18.8 %all-to-all-start.3 = ((bf16[8,256,128]{2,1,0:T(8,128)(2,1)}), bf16[8,256,128]{2,1,0:T(8,128)(2,1)S(1)}, u32[]{:S(2)}, u32[]{:S(2)}) async-start(bf16[8,256,128]{2,1,0:T(8,128)(2,1)} %get-tuple-element.12), calls=%async_computation.3 | async-start | bytes 1048576 | tf_op jit(solution)/shard_map/all_to_all | solution.py:302
  70.6 23.1 %collective-permute-start.3 = (bf16[8,256,128]{2,1,0:T(8,128)(2,1)S(1)}, bf16[8,256,128]{2,1,0:T(8,128)(2,1)}, u32[]{:S(2)}, u32[]{:S(2)}) collective-permute-start(bf16[8,256,128]{2,1,0:T(8,128)(2,1)S(1)} %all_to_all.21.refs_0_), channel_id=1, source_target_pairs={{0,8},{8,0},{16,24},{24,16},{1,9},{9,1},{17,25},{25,17},{2,10},{10... | collective-permute-start | bytes 1572872 | tf_op jit(solution)/shard_map/ppermute | solution.py:299
  72.2 22.1 %collective-permute-start.1 = (bf16[8,256,128]{2,1,0:T(8,128)(2,1)S(1)}, bf16[8,256,128]{2,1,0:T(8,128)(2,1)S(1)}, u32[]{:S(2)}, u32[]{:S(2)}) collective-permute-start(bf16[8,256,128]{2,1,0:T(8,128)(2,1)S(1)} %all_to_all.20.refs_0_), channel_id=1, source_target_pairs={{0,16},{8,24},{16,0},{24,8},{1,17},{9,25},{17,1},{25,9},{2,18},{10... | collective-permute-start | bytes 1572872 | tf_op jit(solution)/shard_map/ppermute | solution.py:299
  85.9 30.1 %copy-start.3 = (bf16[8,256,128]{2,1,0:T(8,128)(2,1)}, bf16[8,256,128]{2,1,0:T(8,128)(2,1)S(1)}, u32[]{:S(2)}) copy-start(bf16[8,256,128]{2,1,0:T(8,128)(2,1)S(1)} %all-to-all-done.3.refs_4_) | copy-start | bytes 1572868
  85.9 44.7 %all-to-all-start.1 = ((bf16[8,256,128]{2,1,0:T(8,128)(2,1)}), bf16[8,256,128]{2,1,0:T(8,128)(2,1)S(1)}, u32[]{:S(2)}, u32[]{:S(2)}) async-start(bf16[8,256,128]{2,1,0:T(8,128)(2,1)} %get-tuple-element.10), calls=%async_computation.1 | async-start | bytes 1048576 | tf_op jit(solution)/shard_map/all_to_all | solution.py:302
  90.6 14.9 %collective-permute-start.4 = (bf16[8,256,128]{2,1,0:T(8,128)(2,1)S(1)}, bf16[8,256,128]{2,1,0:T(8,128)(2,1)S(1)}, u32[]{:S(2)}, u32[]{:S(2)}) collective-permute-start(bf16[8,256,128]{2,1,0:T(8,128)(2,1)S(1)} %all_to_all.21.refs_0_), channel_id=1, source_target_pairs={{0,16},{8,24},{16,0},{24,8},{1,17},{9,25},{17,1},{25,9},{2,18},{10... | collective-permute-start | bytes 1572872 | tf_op jit(solution)/shard_map/ppermute | solution.py:299
  92.2 38.4 %collective-permute-start = (bf16[8,256,128]{2,1,0:T(8,128)(2,1)S(1)}, bf16[8,256,128]{2,1,0:T(8,128)(2,1)S(1)}, u32[]{:S(2)}, u32[]{:S(2)}) collective-permute-start(bf16[8,256,128]{2,1,0:T(8,128)(2,1)S(1)} %all_to_all.20.refs_0_), channel_id=1, source_target_pairs={{0,8},{8,0},{16,24},{24,16},{1,9},{9,1},{17,25},{25,17},{2,10},{10... | collective-permute-start | bytes 1572872 | tf_op jit(solution)/shard_map/ppermute | solution.py:299
  93.7 22.3 %collective-permute-start.5 = (bf16[8,256,128]{2,1,0:T(8,128)(2,1)}, bf16[8,256,128]{2,1,0:T(8,128)(2,1)S(1)}, u32[]{:S(2)}, u32[]{:S(2)}) collective-permute-start(bf16[8,256,128]{2,1,0:T(8,128)(2,1)} %collective-permute-done.3.refs_1_), channel_id=1, source_target_pairs={{0,16},{8,24},{16,0},{24,8},{1,17},{9,25},{17,1},{25,9},{2,18},{10... | collective-permute-start | bytes 1572872 | tf_op jit(solution)/shard_map/ppermute | solution.py:299
  94.2 36.4 %copy-start.4 = (bf16[8,256,128]{2,1,0:T(8,128)(2,1)}, bf16[8,256,128]{2,1,0:T(8,128)(2,1)S(1)}, u32[]{:S(2)}) copy-start(bf16[8,256,128]{2,1,0:T(8,128)(2,1)S(1)} %collective-permute-done.1.refs_2_) | copy-start | bytes 1572868
  94.2 36.4 %collective-permute-start.2 = (bf16[8,256,128]{2,1,0:T(8,128)(2,1)S(1)}, bf16[8,256,128]{2,1,0:T(8,128)(2,1)}, u32[]{:S(2)}, u32[]{:S(2)}) collective-permute-start(bf16[8,256,128]{2,1,0:T(8,128)(2,1)S(1)} %collective-permute-done.1.refs_2_), channel_id=1, source_target_pairs={{0,8},{8,0},{16,24},{24,16},{1,9},{9,1},{17,25},{25,17},{2,10},{10... | collective-permute-start | bytes 1572872 | tf_op jit(solution)/shard_map/ppermute | solution.py:299
  105.5 10.5 %copy-start.6 = (bf16[8,256,128]{2,1,0:T(8,128)(2,1)}, bf16[8,256,128]{2,1,0:T(8,128)(2,1)S(1)}, u32[]{:S(2)}) copy-start(bf16[8,256,128]{2,1,0:T(8,128)(2,1)S(1)} %collective-permute-done.4.refs_2_) | copy-start | bytes 1572868
  116.0 0.8 copy-start.7
  130.6 0.8 copy-start.1
  130.6 1.0 copy-start.5

commit v2 on v1

--- a/solution.py
+++ b/solution.py
@@ -19,6 +19,7 @@
 PAIRS = SUB // 2
 CHUNKS = 2
 JBLOCK = 16
+PITCH = JBLOCK + 4
 
 EPSILON = 1e-06
 
@@ -44,11 +45,30 @@
     return fine.astype(np.float32), coarse.astype(np.float32)
 
 
-def front_kernel(rows_dev, wins, offs, strain, perm, fine, coarse, *rest):
-    outs = rest[: 2 * CHUNKS]
-    high, low, table_high, table_low, spec, laid = rest[2 * CHUNKS :]
+def front_kernel(rows_dev, wins, offs, mesh_row, sources, strain_hbm, fine, coarse, *rest):
+    pieces, perm = rest[: 1 + CHUNKS], rest[1 + CHUNKS]
+    strain, high, low, table_high, table_low, spec, laid, fold, arrived = rest[2 + CHUNKS :]
     chan, _, seg = strain.shape
     bins_dev = NF // wins
+    fetch = pltpu.make_async_copy(strain_hbm, strain, arrived)
+    fetch.start()
+
+    count = sources.shape[1]
+    own = sources[...] - mesh_row[0] * chan
+    channel = lax.broadcasted_iota(jnp.int32, (chan, count), 0)
+    match = jnp.where(own == channel, 1.0, 0.0)
+    hit = jnp.sum(match, axis=1, keepdims=True)
+    before = lax.broadcasted_iota(jnp.int32, (chan, chan), 1)
+    after = lax.broadcasted_iota(jnp.int32, (chan, chan), 0)
+    earlier = jnp.where(before < after, 1.0, 0.0).astype(jnp.bfloat16)
+    ahead = jnp.sum(
+        jnp.dot(earlier, match.astype(jnp.bfloat16), preferred_element_type=jnp.float32),
+        axis=1,
+        keepdims=True,
+    )
+    here = after[:, :1].astype(jnp.float32)
+    slot = jnp.where(hit > 0.0, ahead, jnp.sum(hit) + here - ahead)
+    perm[...] = jnp.where(slot == before.astype(jnp.float32), 1.0, 0.0).astype(jnp.bfloat16)
 
     for parity in range(2):
         for part in range(2):
@@ -66,35 +86,53 @@
                 ).astype(jnp.bfloat16)
 
     edge = NT // 16
-    place = lax.broadcasted_iota(jnp.int32, (8, seg), 1)
-    number = lax.broadcasted_iota(jnp.int32, (8, seg), 0)
-    begin = jnp.zeros((8, seg), jnp.int32)
+    tiles = seg // LANES
+    number = lax.broadcasted_iota(jnp.int32, (8, LANES), 0) % rows_dev
+    begin = jnp.zeros((8, LANES), jnp.int32)
     for r in range(rows_dev):
         begin = jnp.where(number == r, offs[r], begin)
-    sample = place - begin
-    inside = (sample >= 0) & (sample < NT)
-    near = jnp.minimum(sample, NT - 1 - sample).astype(jnp.float32) + 0.5
-    slope = 0.5 * (1.0 - jnp.cos(near * (math.pi / edge)))
-    taper = jnp.where(inside, jnp.where(near < edge, slope, 1.0), 0.0)
-    window = jnp.where(inside, 1.0, 0.0)
-
-    step_rows = 16
+    taper, window = {}, {}
+    for tile in (0, 1, tiles - 2, tiles - 1):
+        sample = lax.broadcasted_iota(jnp.int32, (8, LANES), 1) + tile * LANES - begin
+        inside = (sample >= 0) & (sample < NT)
+        near = jnp.minimum(sample, NT - 1 - sample).astype(jnp.float32) + 0.5
+        slope = 0.5 * (1.0 - jnp.cos(near * (math.pi / edge)))
+        taper[tile] = jnp.where(inside, jnp.where(near < edge, slope, 1.0), 0.0)
+        window[tile] = jnp.where(inside, 1.0, 0.0)
+
+    step_chan = 16
+    step_rows = step_chan * rows_dev
+    half_tiles = HALF // LANES
+    fetch.wait()
 
     def prepare(i, carry):
-        at = pl.ds(pl.multiple_of(i * step_rows, step_rows), step_rows)
-        for r in range(rows_dev):
-            x = strain[at, r, :].astype(jnp.float32)
-            mean = jnp.sum(x * window[r : r + 1], axis=1, keepdims=True) * (1.0 / NT)
-            z = (x - mean) * taper[r : r + 1]
-            first = jnp.concatenate((z[:, : seg - NT] + z[:, NT:], z[:, seg - NT : HALF]), axis=1)
-            second = z[:, HALF:NT]
-            for parity, folded in enumerate((first + second, first - second)):
-                top = folded.astype(jnp.bfloat16)
-                high[r, parity, at, :] = top
-                low[r, parity, at, :] = (folded - top.astype(jnp.float32)).astype(jnp.bfloat16)
+        at = pl.ds(pl.multiple_of(i * step_chan, step_chan), step_chan)
+        x = strain[at].astype(jnp.float32).reshape(step_rows // 8, 8, seg)
+        x = [x[:, :, t * LANES : (t + 1) * LANES] for t in range(tiles)]
+        total = x[0] * window[0] + x[tiles - 1] * window[tiles - 1]
+        for t in range(1, tiles - 1):
+            total = total + x[t]
+        mean = jnp.sum(total, axis=2, keepdims=True) * (1.0 / NT)
+        z = [v - mean for v in x]
+        for t in taper:
+            z[t] = z[t] * taper[t]
+        z[0] = z[0] + z[tiles - 1]
+        for t in range(half_tiles):
+            fold[0, t] = (z[t] + z[t + half_tiles]).reshape(step_rows, LANES)
+            fold[1, t] = (z[t] - z[t + half_tiles]).reshape(step_rows, LANES)
+        for parity in range(2):
+            for t in range(half_tiles):
+                lanes = pl.ds(t * LANES, LANES)
+                for r in range(rows_dev):
+                    value = fold[parity, t, pl.ds(r, step_chan, stride=rows_dev), :]
+                    top = value.astype(jnp.bfloat16)
+                    high[r, parity, at, lanes] = top
+                    low[r, parity, at, lanes] = (value - top.astype(jnp.float32)).astype(
+                        jnp.bfloat16
+                    )
         return carry
 
-    lax.fori_loop(0, chan // step_rows, prepare, 0)
+    lax.fori_loop(0, chan // step_chan, prepare, 0)
 
     rows = NBAND * SUB
     for r in range(rows_dev):
@@ -136,48 +174,64 @@
                     real = spec[parity, pl.ds(band * SUB, PAIRS), lanes] * scale_l
                     imag = spec[parity, pl.ds(band * SUB + PAIRS, PAIRS), lanes] * scale_l
                     for part, value in enumerate((real * cos - imag * sin, real * sin + imag * cos)):
-                        start = band * SUB * 2 * rows_dev + parity * 2 * rows_dev + part * rows_dev + r
-                        laid[lane, pl.ds(start, PAIRS, stride=4 * rows_dev), :] = value
+                        start = band * PAIRS * PITCH + (2 * parity + part) * rows_dev + r
+                        laid[lane, pl.ds(start, PAIRS, stride=PITCH), :] = value
 
     per_win = bins_dev * 2 * rows_dev
+    pair_rows = 4 * rows_dev
     per_chunk = per_win // CHUNKS
-
-    def emit(w, carry):
-        at = pl.ds(pl.multiple_of(w * per_win, per_win), per_win)
+    for w in range(wins):
         white = jnp.concatenate(
-            [laid[lane, at, :].astype(jnp.bfloat16) for lane in range(chan // LANES)], axis=1
+            [
+                jnp.concatenate(
+                    [
+                        laid[lane, pl.ds((w * bins_dev // 2 + i) * PITCH, pair_rows), :].astype(
+                            jnp.bfloat16
+                        )
+                        for i in range(bins_dev // 2)
+                    ],
+                    axis=0,
+                )
+                for lane in range(chan // LANES)
+            ],
+            axis=1,
         )
         placed = jnp.dot(white, perm[...], preferred_element_type=jnp.float32).astype(jnp.bfloat16)
         for k in range(CHUNKS):
-            piece = placed[k * per_chunk : (k + 1) * per_chunk]
-            for half in range(2):
-                outs[2 * k + half][w] = piece[:, half * LANES : (half + 1) * LANES]
-        return carry
-
-    lax.fori_loop(0, wins, emit, 0)
-
-
-def front(strain, offsets, perm, wins):
+            pieces[k][w] = placed[k * per_chunk : (k + 1) * per_chunk, :LANES]
+        pieces[CHUNKS][w] = placed[:, LANES:]
+
+
+def front(strain, sources, offsets, mesh_row, wins):
     chan, rows_dev, seg = strain.shape
-    rows = NF // wins * 2 * rows_dev // CHUNKS
+    rows = NF // wins * 2 * rows_dev
     fine, coarse = table_parts()
     vmem = pl.BlockSpec(memory_space=pltpu.VMEM)
+    smem = pl.BlockSpec(memory_space=pltpu.SMEM)
+    part = jax.ShapeDtypeStruct((wins, rows // CHUNKS, LANES), jnp.bfloat16)
     return pl.pallas_call(
         functools.partial(front_kernel, rows_dev, wins),
-        out_shape=[jax.ShapeDtypeStruct((wins, rows, LANES), jnp.bfloat16)] * (2 * CHUNKS),
-        in_specs=[pl.BlockSpec(memory_space=pltpu.SMEM)] + [vmem] * 4,
-        out_specs=[vmem] * (2 * CHUNKS),
+        out_shape=[part] * CHUNKS
+        + [
+            jax.ShapeDtypeStruct((wins, rows, LANES), jnp.bfloat16),
+            jax.ShapeDtypeStruct((chan, chan), jnp.bfloat16),
+        ],
+        in_specs=[smem, smem, vmem, pl.BlockSpec(memory_space=pl.ANY), vmem, vmem],
+        out_specs=[vmem] * (CHUNKS + 2),
         scratch_shapes=[
+            pltpu.VMEM(strain.shape, strain.dtype),
             pltpu.VMEM((rows_dev, 2, chan, HALF), jnp.bfloat16),
             pltpu.VMEM((rows_dev, 2, chan, HALF), jnp.bfloat16),
             pltpu.VMEM((2, NBAND, SUB, HALF), jnp.bfloat16),
             pltpu.VMEM((2, NBAND, SUB, HALF), jnp.bfloat16),
             pltpu.VMEM((2, NBAND * SUB, chan), jnp.float32),
-            pltpu.VMEM((chan // LANES, NF * 2 * rows_dev, LANES), jnp.float32),
+            pltpu.VMEM((chan // LANES, NBAND * PAIRS * PITCH, LANES), jnp.float32),
+            pltpu.VMEM((2, HALF // LANES, 16 * rows_dev, LANES), jnp.float32),
+            pltpu.SemaphoreType.DMA,
         ],
         compiler_params=pltpu.CompilerParams(vmem_limit_bytes=56 * 2**20),
         name="front",
-    )(offsets, strain, perm, jnp.asarray(fine), jnp.asarray(coarse))
+    )(offsets, mesh_row, sources, strain, jnp.asarray(fine), jnp.asarray(coarse))
 
 
 def cross_kernel(rows_dev, wins, records, *refs):
@@ -223,33 +277,34 @@
             product = jnp.dot(both, receivers, preferred_element_type=jnp.float32)
             for part in range(2):
                 for half in range(product.shape[1] // LANES):
-                    laid[part, half, pl.ds(g * group + b, sources, stride=JBLOCK), :] = product[
+                    laid[part, half, pl.ds(g * group + b, sources, stride=PITCH), :] = product[
                         part * sources : (part + 1) * sources, half * LANES : (half + 1) * LANES
                     ]
 
-    few = 16
+    few = 32
 
     def emit(i, carry):
-        rows = pl.ds(pl.multiple_of(i * few * JBLOCK, few * JBLOCK), few * JBLOCK)
-        at = pl.ds(pl.multiple_of(i * few, few), few)
-        for part in range(2):
-            for half in range(laid.shape[1]):
-                value = (laid[part, half, rows, :] * scale).astype(jnp.bfloat16)
-                out[part, at, :, half * LANES : (half + 1) * LANES] = value.reshape(few, JBLOCK, LANES)
+        for n in range(few):
+            rows = pl.ds((i * few + n) * PITCH, JBLOCK)
+            for part in range(2):
+                for half in range(laid.shape[1]):
+                    value = (laid[part, half, rows, :] * scale).astype(jnp.bfloat16)
+                    out[part, i * few + n, :, half * LANES : (half + 1) * LANES] = value
         return carry
 
     lax.fori_loop(0, sources // few, emit, 0)
 
 
 def cross(k, whole, owners, other, perm, select, shape, records, rows_dev):
-    wins, rows, _ = other.shape
+    wins, rows, _ = owners[0].shape
     sources, chan = shape[1], shape[3]
     per_block = JBLOCK * 2 * rows_dev
     steps = rows // per_block
     piece = pl.BlockSpec((wins, per_block, LANES), lambda g: (0, g, 0))
+    later = pl.BlockSpec((wins, per_block, LANES), lambda g: (0, k * steps + g, 0))
     fixed = lambda array: pl.BlockSpec(array.shape, lambda g: (0, 0))
     args = list(owners) + [other, perm, select]
-    specs = [piece] * (len(owners) + 1) + [fixed(perm), fixed(select)]
+    specs = [piece] * len(owners) + [later, fixed(perm), fixed(select)]
     body = functools.partial(cross_kernel, rows_dev, wins, records)
     aliases = {}
     if whole is not None:
@@ -264,7 +319,7 @@
         out_shape=jax.ShapeDtypeStruct(shape, jnp.bfloat16),
         in_specs=specs,
         out_specs=pl.BlockSpec((2, sources, JBLOCK, chan), lambda g: (0, 0, k * steps + g, 0)),
-        scratch_shapes=[pltpu.VMEM((2, chan // LANES, sources * JBLOCK, LANES), jnp.float32)],
+        scratch_shapes=[pltpu.VMEM((2, chan // LANES, sources * PITCH, LANES), jnp.float32)],
         input_output_aliases=aliases,
         compiler_params=pltpu.CompilerParams(vmem_limit_bytes=56 * 2**20),
         name=f"cross{k}",
@@ -274,12 +329,6 @@
 def body(recs, wins, strain, sources, offsets):
     chan, rows_dev, _ = strain.shape
     me = lax.axis_index("rec")
-    channel = jnp.arange(chan, dtype=jnp.int32)
-    local = sources - me * chan
-    hit = jnp.any(local[None, :] == channel[:, None], axis=1).astype(jnp.int32)
-    ahead = jnp.sum(jnp.where(channel[None, :] < channel[:, None], hit[None, :], 0), axis=1)
-    slot = jnp.where(hit > 0, ahead, jnp.sum(hit) + channel - ahead)
-    perm = (slot[:, None] == channel[None, :]).astype(jnp.bfloat16)
     owner = sources // chan
     rank = jnp.sum(
         (owner[None, :] == owner[:, None]) & (sources[None, :] < sources[:, None]), axis=1
@@ -293,7 +342,7 @@
         (owner[:, None, None] == order[None, :, None]) & (rank[:, None, None] == place[None, None, :])
     ).astype(jnp.bfloat16).reshape(sources.shape[0], recs * LANES)
 
-    pieces = front(strain, offsets, perm, wins)
+    *pieces, perm = front(strain, sources[None], offsets, me.astype(jnp.int32)[None], wins)
 
     def swap(array, bit):
         return lax.ppermute(array, "rec", [(i, i ^ bit) for i in range(recs)])
@@ -303,7 +352,7 @@
 
     owners = []
     for k in range(CHUNKS):
-        mine = spread(pieces[2 * k])
+        mine = spread(pieces[k])
         if recs == 4:
             along_x, along_y = swap(mine, 1), swap(mine, 2)
             far = swap(along_x, 2) if k % 2 == 0 else swap(along_y, 1)
@@ -311,10 +360,10 @@
         else:
             gathered = lax.all_gather(mine, "rec", axis=0)
             owners.append((mine,) + tuple(gathered[i] for i in range(recs)))
+    other = spread(pieces[CHUNKS])
     shape = (2, sources.shape[0], NF // wins, chan)
     whole = None
     for k in range(CHUNKS):
-        other = spread(pieces[2 * k + 1])
         whole = cross(k, whole, owners[k], other, perm, select, shape, rows_dev * wins, rows_dev)
     return whole
 

time: 146 us -> 120 us (0.82)
  Pallas kernels: 51.3 us -> 37 us
  waiting for transfers between devices: 32.2 us -> 27.7 us
  starting transfers between devices: 14.4 us -> 10.9 us
  other arithmetic: 4.49 us -> 2.2 us
    all_to_all x2 -> x1, waiting for transfers between devices: 12.2 us -> 0.01 us  [spread(): return lax.all_to_all(array, 'win', split_axis=0, concat_axis=0, tiled=True)]
    pallas_call x2, Pallas kernels: 27.6 us -> 19.3 us  [cross(): pl.pallas_call(body, grid=(steps,), out_shape=jax.ShapeDtypeStruct(shape,...]
    ppermute x6, waiting for transfers between devices: 20 us -> 27.7 us  [swap(): return lax.ppermute(array, 'rec', [(i, i ^ bit) for i in range(recs)])]
    pallas_call x1, Pallas kernels: 23.7 us -> 17.8 us  [front(): pl.pallas_call(functools.partial(front_kernel, rows_dev, wins), out_shape...]
    all_to_all x2 -> x1, starting transfers between devices: 7.16 us -> 3.74 us  [spread(): return lax.all_to_all(array, 'win', split_axis=0, concat_axis=0, tiled=True)]
  transfers between devices with their start and end apart: 8 -> 7, of which waited for: 3 -> 3; matrix products, arithmetic and copies ran while one was open for 2% -> 2% of each run, Pallas kernels for 9% -> 8%
where the time goes in v2:
time: 120 us
  blocking collectives  40.4 us (34%)
  Pallas kernels  37 us (31%)
  waiting for transfers between devices  27.7 us (23%)
  starting transfers between devices  10.9 us (9%)
  other arithmetic  2.2 us (2%)
  local copies, waits for them, and re-layouts  1.53 us (1%)
    all_to_all x2, blocking collectives, spread(): return lax.all_to_all(array, 'win', split_axis=0, concat_axis=0, tiled=True)  40.4 us
    ppermute x6, waiting for transfers between devices, swap(): return lax.ppermute(array, 'rec', [(i, i ^ bit) for i in range(recs)])  27.7 us
    pallas_call x2, Pallas kernels, cross(): pl.pallas_call(body, grid=(steps,), out_shape=jax.ShapeDtypeStruct(shape,...  19.3 us
    pallas_call x1, Pallas kernels, front(): pl.pallas_call(functools.partial(front_kernel, rows_dev, wins), out_shape...  17.8 us
    ppermute x6, starting transfers between devices, swap(): return lax.ppermute(array, 'rec', [(i, i ^ bit) for i in range(recs)])  7.19 us
    all_to_all x1, starting transfers between devices, spread(): return lax.all_to_all(array, 'win', split_axis=0, concat_axis=0, tiled=True)  3.74 us
  transfers between devices with their start and end apart: 7, of which 3 were waited for; matrix products, arithmetic and copies ran while one was open for 2% of the time, Pallas kernels for 8%

profile of v2, /device:TPU:0, one launch (start us, length us, event | category | flops | bytes accessed | tf_op | source)
XLA Modules:
  0.0 119.9 jit_solution(7356072127201939018)
XLA Ops:
  0.0 17.8 %front.1 = (bf16[8,256,128]{2,1,0:T(8,128)(2,1)}, bf16[8,256,128]{2,1,0:T(8,128)(2,1)}, bf16[8,512,128]{2,1,0:T(8,128)(2,1)}, bf16[256,256]{1,0:T(8,128)(2,1)}) custom-call(s32[4]{0:T(128)} %offs.1, s32[1]{0:T(128)} %bitcast.mesh_row, s32[1,256]{1,0:T(1,128)} %bitcast.9, bf16[256,4,2176]{2,1,0:T(4,128)(2,1)} %strain_hbm.1, ...), custom_call_target="tpu_custom_call" | custom-call | tf_op jit(solution)/shard_map/front/pallas_call | solution.py:212
  17.8 21.7 %all_to_all.15.refs_0_ = bf16[8,256,128]{2,1,0:T(8,128)(2,1)S(1)} all-to-all(bf16[8,256,128]{2,1,0:T(8,128)(2,1)} %get-tuple-element.9), channel_id=1, replica_groups=mesh['rec'=4,'win'=8] {'win'}, dimensions={0} | all-to-all | bytes 1048576 | tf_op jit(solution)/shard_map/all_to_all | solution.py:351
  39.5 0.0 copy-start.1
  39.5 18.7 %all_to_all.16.refs_0_ = bf16[8,256,128]{2,1,0:T(8,128)(2,1)S(1)} all-to-all(bf16[8,256,128]{2,1,0:T(8,128)(2,1)} %get-tuple-element.12), channel_id=1, replica_groups=mesh['rec'=4,'win'=8] {'win'}, dimensions={0} | all-to-all | bytes 1048576 | tf_op jit(solution)/shard_map/all_to_all | solution.py:351
  58.2 0.0 copy-start.2
  58.2 3.7 %all-to-all-start.1 = ((bf16[8,512,128]{2,1,0:T(8,128)(2,1)}), bf16[8,512,128]{2,1,0:T(8,128)(2,1)S(1)}, u32[]{:S(2)}, u32[]{:S(2)}) async-start(bf16[8,512,128]{2,1,0:T(8,128)(2,1)} %get-tuple-element.10), calls=%async_computation.1 | async-start | bytes 2097152 | tf_op jit(solution)/shard_map/all_to_all | solution.py:351
  61.9 1.6 %collective-permute-start.3 = (bf16[8,256,128]{2,1,0:T(8,128)(2,1)S(1)}, bf16[8,256,128]{2,1,0:T(8,128)(2,1)}, u32[]{:S(2)}, u32[]{:S(2)}) collective-permute-start(bf16[8,256,128]{2,1,0:T(8,128)(2,1)S(1)} %all_to_all.16.refs_0_), channel_id=1, source_target_pairs={{0,8},{8,0},{16,24},{24,16},{1,9},{9,1},{17,25},{25,17},{2,10},{10... | collective-permute-start | bytes 1572872 | tf_op jit(solution)/shard_map/ppermute | solution.py:348
  63.5 1.5 %collective-permute-start.1 = (bf16[8,256,128]{2,1,0:T(8,128)(2,1)S(1)}, bf16[8,256,128]{2,1,0:T(8,128)(2,1)S(1)}, u32[]{:S(2)}, u32[]{:S(2)}) collective-permute-start(bf16[8,256,128]{2,1,0:T(8,128)(2,1)S(1)} %all_to_all.15.refs_0_), channel_id=1, source_target_pairs={{0,16},{8,24},{16,0},{24,8},{1,17},{9,25},{17,1},{25,9},{2,18},{10... | collective-permute-start | bytes 1572872 | tf_op jit(solution)/shard_map/ppermute | solution.py:348
  65.0 0.7 and_select_fusion
  65.7 1.0 convert_reduce_fusion
  66.7 0.1 iota_compare_fusion
  66.8 0.6 collective-permute-start.4
  67.3 0.5 collective-permute-start
  67.9 9.0 %collective-permute-done.3.refs_1_ = bf16[8,256,128]{2,1,0:T(8,128)(2,1)} collective-permute-done((bf16[8,256,128]{2,1,0:T(8,128)(2,1)S(1)}, bf16[8,256,128]{2,1,0:T(8,128)(2,1)}, u32[]{:S(2)}, u32[]{:S(2)}) %collective-permute-start.3) | collective-permute-done | bytes 524320 | tf_op jit(solution)/shard_map/ppermute | solution.py:348
  76.9 1.5 %collective-permute-start.5 = (bf16[8,256,128]{2,1,0:T(8,128)(2,1)}, bf16[8,256,128]{2,1,0:T(8,128)(2,1)}, u32[]{:S(2)}, u32[]{:S(2)}) collective-permute-start(bf16[8,256,128]{2,1,0:T(8,128)(2,1)} %collective-permute-done.3.refs_1_), channel_id=1, source_target_pairs={{0,16},{8,24},{16,0},{24,8},{1,17},{9,25},{17,1},{25,9},{2,18},{10... | collective-permute-start | bytes 1572872 | tf_op jit(solution)/shard_map/ppermute | solution.py:348
  78.4 0.0 collective-permute-done.1.refs_2_
  78.4 1.5 %collective-permute-start.2 = (bf16[8,256,128]{2,1,0:T(8,128)(2,1)S(1)}, bf16[8,256,128]{2,1,0:T(8,128)(2,1)}, u32[]{:S(2)}, u32[]{:S(2)}) collective-permute-start(bf16[8,256,128]{2,1,0:T(8,128)(2,1)S(1)} %collective-permute-done.1.refs_2_), channel_id=1, source_target_pairs={{0,8},{8,0},{16,24},{24,16},{1,9},{9,1},{17,25},{25,17},{2,10},{10... | collective-permute-start | bytes 1572872 | tf_op jit(solution)/shard_map/ppermute | solution.py:348
  79.9 0.1 broadcast_compare_fusion
  80.0 0.3 and_convert_fusion
  80.4 0.7 copy.9
  81.1 8.5 %collective-permute-done.4.refs_2_ = bf16[8,256,128]{2,1,0:T(8,128)(2,1)} collective-permute-done((bf16[8,256,128]{2,1,0:T(8,128)(2,1)S(1)}, bf16[8,256,128]{2,1,0:T(8,128)(2,1)}, u32[]{:S(2)}, u32[]{:S(2)}) %collective-permute-start.4) | collective-permute-done | bytes 524320 | tf_op jit(solution)/shard_map/ppermute | solution.py:348
  89.6 0.0 all-to-all-done.1.refs_4_
  89.6 10.1 %collective-permute-done.5.refs_3_ = bf16[8,256,128]{2,1,0:T(8,128)(2,1)} collective-permute-done((bf16[8,256,128]{2,1,0:T(8,128)(2,1)}, bf16[8,256,128]{2,1,0:T(8,128)(2,1)}, u32[]{:S(2)}, u32[]{:S(2)}) %collective-permute-start.5) | collective-permute-done | bytes 524320 | tf_op jit(solution)/shard_map/ppermute | solution.py:348
  99.8 0.0 copy-done.2
  99.8 0.0 copy-done
  99.8 9.6 %cross0.1.refs_7_ = bf16[2,256,64,256]{3,2,1,0:T(8,128)(2,1)} custom-call(bf16[8,256,128]{2,1,0:T(8,128)(2,1)} %copy-done.2, bf16[8,256,128]{2,1,0:T(8,128)(2,1)} %collective-permute-done.3.refs_1_, bf16[8,256,128]{2,1,0:T(8,128)(2,1)} %collective-permute-done.4.refs_2_, bf16[8,256,128]{2,1,0:T(8,128)(2,1)} %collective-permute-done.5.refs_3_, ...), custom_call_target="tpu_custom_call" | custom-call | tf_op jit(solution)/shard_map/cross0/pallas_call | solution.py:316
  109.4 0.0 collective-permute-done.refs_1_
  109.4 0.0 collective-permute-done.2.refs_3_
  109.4 0.0 copy-done.1
  109.4 0.0 copy-done.3
  109.5 0.8 copy-done.4
  110.2 9.6 %cross1.1 = bf16[2,256,64,256]{3,2,1,0:T(8,128)(2,1)} custom-call(bf16[8,256,128]{2,1,0:T(8,128)(2,1)} %copy-done.1, bf16[8,256,128]{2,1,0:T(8,128)(2,1)} %copy-done.4, bf16[8,256,128]{2,1,0:T(8,128)(2,1)} %copy-done.3, bf16[8,256,128]{2,1,0:T(8,128)(2,1)} %collective-permute-done.2.refs_3_, ...), custom_call_target="tpu_custom_call", output_to_operand_aliasing={{}: (7, {})} | custom-call | tf_op jit(solution)/shard_map/cross1/pallas_call | solution.py:316
  (4 shorter events, 0.0 us)
Async XLA Ops:
  39.5 70.0 %copy-start.1 = (bf16[8,256,128]{2,1,0:T(8,128)(2,1)}, bf16[8,256,128]{2,1,0:T(8,128)(2,1)S(1)}, u32[]{:S(2)}) copy-start(bf16[8,256,128]{2,1,0:T(8,128)(2,1)S(1)} %all_to_all.15.refs_0_) | copy-start | bytes 1572868
  58.2 41.6 %copy-start.2 = (bf16[8,256,128]{2,1,0:T(8,128)(2,1)}, bf16[8,256,128]{2,1,0:T(8,128)(2,1)S(1)}, u32[]{:S(2)}) copy-start(bf16[8,256,128]{2,1,0:T(8,128)(2,1)S(1)} %all_to_all.16.refs_0_) | copy-start | bytes 1572868
  58.2 31.4 %all-to-all-start.1 = ((bf16[8,512,128]{2,1,0:T(8,128)(2,1)}), bf16[8,512,128]{2,1,0:T(8,128)(2,1)S(1)}, u32[]{:S(2)}, u32[]{:S(2)}) async-start(bf16[8,512,128]{2,1,0:T(8,128)(2,1)} %get-tuple-element.10), calls=%async_computation.1 | async-start | bytes 2097152 | tf_op jit(solution)/shard_map/all_to_all | solution.py:351
  61.9 15.0 %collective-permute-start.3 = (bf16[8,256,128]{2,1,0:T(8,128)(2,1)S(1)}, bf16[8,256,128]{2,1,0:T(8,128)(2,1)}, u32[]{:S(2)}, u32[]{:S(2)}) collective-permute-start(bf16[8,256,128]{2,1,0:T(8,128)(2,1)S(1)} %all_to_all.16.refs_0_), channel_id=1, source_target_pairs={{0,8},{8,0},{16,24},{24,16},{1,9},{9,1},{17,25},{25,17},{2,10},{10... | collective-permute-start | bytes 1572872 | tf_op jit(solution)/shard_map/ppermute | solution.py:348
  63.5 14.9 %collective-permute-start.1 = (bf16[8,256,128]{2,1,0:T(8,128)(2,1)S(1)}, bf16[8,256,128]{2,1,0:T(8,128)(2,1)S(1)}, u32[]{:S(2)}, u32[]{:S(2)}) collective-permute-start(bf16[8,256,128]{2,1,0:T(8,128)(2,1)S(1)} %all_to_all.15.refs_0_), channel_id=1, source_target_pairs={{0,16},{8,24},{16,0},{24,8},{1,17},{9,25},{17,1},{25,9},{2,18},{10... | collective-permute-start | bytes 1572872 | tf_op jit(solution)/shard_map/ppermute | solution.py:348
  66.8 22.8 %collective-permute-start.4 = (bf16[8,256,128]{2,1,0:T(8,128)(2,1)S(1)}, bf16[8,256,128]{2,1,0:T(8,128)(2,1)}, u32[]{:S(2)}, u32[]{:S(2)}) collective-permute-start(bf16[8,256,128]{2,1,0:T(8,128)(2,1)S(1)} %all_to_all.16.refs_0_), channel_id=1, source_target_pairs={{0,16},{8,24},{16,0},{24,8},{1,17},{9,25},{17,1},{25,9},{2,18},{10... | collective-permute-start | bytes 1572872 | tf_op jit(solution)/shard_map/ppermute | solution.py:348
  67.3 42.1 %collective-permute-start = (bf16[8,256,128]{2,1,0:T(8,128)(2,1)S(1)}, bf16[8,256,128]{2,1,0:T(8,128)(2,1)S(1)}, u32[]{:S(2)}, u32[]{:S(2)}) collective-permute-start(bf16[8,256,128]{2,1,0:T(8,128)(2,1)S(1)} %all_to_all.15.refs_0_), channel_id=1, source_target_pairs={{0,8},{8,0},{16,24},{24,16},{1,9},{9,1},{17,25},{25,17},{2,10},{10... | collective-permute-start | bytes 1572872 | tf_op jit(solution)/shard_map/ppermute | solution.py:348
  76.9 22.9 %collective-permute-start.5 = (bf16[8,256,128]{2,1,0:T(8,128)(2,1)}, bf16[8,256,128]{2,1,0:T(8,128)(2,1)}, u32[]{:S(2)}, u32[]{:S(2)}) collective-permute-start(bf16[8,256,128]{2,1,0:T(8,128)(2,1)} %collective-permute-done.3.refs_1_), channel_id=1, source_target_pairs={{0,16},{8,24},{16,0},{24,8},{1,17},{9,25},{17,1},{25,9},{2,18},{10... | collective-permute-start | bytes 1572872 | tf_op jit(solution)/shard_map/ppermute | solution.py:348
  78.4 31.0 %copy-start.3 = (bf16[8,256,128]{2,1,0:T(8,128)(2,1)}, bf16[8,256,128]{2,1,0:T(8,128)(2,1)S(1)}, u32[]{:S(2)}) copy-start(bf16[8,256,128]{2,1,0:T(8,128)(2,1)S(1)} %collective-permute-done.1.refs_2_) | copy-start | bytes 1572868
  78.4 31.0 %collective-permute-start.2 = (bf16[8,256,128]{2,1,0:T(8,128)(2,1)S(1)}, bf16[8,256,128]{2,1,0:T(8,128)(2,1)}, u32[]{:S(2)}, u32[]{:S(2)}) collective-permute-start(bf16[8,256,128]{2,1,0:T(8,128)(2,1)S(1)} %collective-permute-done.1.refs_2_), channel_id=1, source_target_pairs={{0,8},{8,0},{16,24},{24,16},{1,9},{9,1},{17,25},{25,17},{2,10},{10... | collective-permute-start | bytes 1572872 | tf_op jit(solution)/shard_map/ppermute | solution.py:348
  89.6 10.2 %copy-start = (bf16[8,512,128]{2,1,0:T(8,128)(2,1)}, bf16[8,512,128]{2,1,0:T(8,128)(2,1)S(1)}, u32[]{:S(2)}) copy-start(bf16[8,512,128]{2,1,0:T(8,128)(2,1)S(1)} %all-to-all-done.1.refs_4_) | copy-start | bytes 3145732
  109.4 0.8 copy-start.4
